TPU v7x, 256 devices: a whole 4x4x8 slice. The times are simulated.
256 devices in a mesh: space: 16 (over z, core), mode: 16 (over y, x).
Axes of the slice: x: 4, y: 4, z: 8, core: 2. Of those that a mesh axis runs over, the one named last changes fastest.
Arguments:
- guess: float32 [8192, 2048], P('space', 'mode'), may hold values from -6 to 6
- forcing: float32 [8192, 2048], P('space', 'mode'), may hold values from -6 to 6
- spatial_diag: bfloat16 [8192, 512], P('space'), may hold values from -0.25 to 0.25
- spatial_ghost: bfloat16 [8192, 256], P('space'), may hold values from -0.375 to 0.375
- ghost_rows: int32 [32, 128], P('space'), may hold values from 0 to 511, as said below
- chaos_vals: bfloat16 [128, 128, 128], P('mode'), may hold values from -0.25 to 0.25
- chaos_targets: int32 [16, 8], replicated, may hold values from 0 to 15, as said below
- chaos_count: int32 [16], replicated, may hold values from 1 to 8, as said below
- mean_inverse: bfloat16 [2048, 2048], replicated, may hold values from -0.125 to 0.125
Outputs:
- field: float32 [8192, 2048], P('space', 'mode')
Inputs may be any that keep to these rules, and one draw needn't show every extreme that they name: `ghost_rows`: each row holds 128 distinct node numbers, 0 and 511 among them. `chaos_targets`: the targets in a row are distinct and the first is the row's own chaos block. Only the first chaos_count[j] slots of row j are used; some row uses all 8 slots and some row only one.
All inputs are finite; a program needn't handle non-finite values.
Results may differ from a plain program's by a relative error of at most 0.0021.
Values may be sent and summed in bfloat16 or wider, within the bound.
A program may use at most 128 MiB of HBM per device.

v0:
```python
import jax
import jax.numpy as jnp
from jax import lax
from jax.sharding import Mesh
from jax.sharding import PartitionSpec as P

ITERS = 3
SPACE = ("space_0", "space_1")
MODE = ("mode_0", "mode_1")
SPACE_MODE = ("space_0", "space_1", "mode_0", "mode_1")
step_gain = 0.5


def with_halo(cells, sides, width):
    for axis, dim in sides:
        count = lax.axis_size(axis)
        ends = count - 1
        head = lax.slice_in_dim(cells, 0, width, axis=dim)
        tail = lax.slice_in_dim(cells, cells.shape[dim] - width, cells.shape[dim], axis=dim)
        cells = jnp.concatenate(
            [
                lax.ppermute(tail, axis, [(i, (i + 1) % count) for i in range(ends)]),
                cells,
                lax.ppermute(head, axis, [((i + 1) % count, i) for i in range(ends)]),
            ],
            axis=dim,
        )
    return cells


def one_axis_at_a_time(value, axes):
    for axis in axes:
        value = lax.psum(value, axis)
    return value


def shards(
    guess,
    forcing,
    spatial_diag,
    spatial_ghost,
    ghost_rows,
    chaos_vals,
    chaos_targets,
    chaos_count,
    mean_inverse,
):
    node_rows, local_modes = guess.shape
    ghost_width = ghost_rows.shape[1]
    block_width = chaos_vals.shape[1]
    list_slots = chaos_targets.shape[1]
    all_blocks = chaos_targets.shape[0]
    total_cells = node_rows * lax.axis_size(SPACE) * local_modes * lax.axis_size(MODE)
    slab_tables = lax.all_gather(chaos_vals, MODE, axis=0, tiled=True)
    slab_tables = slab_tables.reshape(all_blocks, list_slots, block_width, block_width)
    slot_used = jnp.arange(list_slots, dtype=jnp.int32)[None, :] < chaos_count[:, None]
    every_block = jnp.arange(all_blocks, dtype=jnp.int32)
    target_hits = (chaos_targets[:, :, None] == every_block[None, None, :]) & slot_used[:, :, None]
    target_hits = target_hits.astype(jnp.bfloat16)
    full_table = jnp.einsum(
        "jsba,jst->jatb", slab_tables, target_hits, preferred_element_type=jnp.float32
    )
    full_table = full_table.astype(jnp.bfloat16).reshape(
        all_blocks * block_width, all_blocks * block_width
    )
    field = guess
    for iteration in range(ITERS):
        field_bf = field.astype(jnp.bfloat16)
        lower_sent = field_bf[ghost_rows[0]]
        upper_sent = field_bf[ghost_rows[1]]
        padded = with_halo(
            jnp.concatenate([lower_sent, upper_sent], axis=0), ((SPACE, 0),), ghost_width
        )
        ghosts = jnp.concatenate([padded[:ghost_width], padded[3 * ghost_width :]], axis=0)
        spatial = jnp.dot(spatial_diag, field_bf, preferred_element_type=jnp.float32)
        spatial = spatial + jnp.dot(spatial_ghost, ghosts, preferred_element_type=jnp.float32)
        field_slab = lax.all_to_all(field_bf, MODE, split_axis=0, concat_axis=1, tiled=True)
        partial_slab = lax.all_to_all(
            forcing - spatial, MODE, split_axis=0, concat_axis=1, tiled=True
        )
        coupled_slab = jnp.dot(field_slab, full_table, preferred_element_type=jnp.float32)
        residual_slab = (partial_slab - coupled_slab).astype(jnp.bfloat16)
        update_slab = lax.dot_general(
            residual_slab,
            mean_inverse,
            (((1,), (1,)), ((), ())),
            preferred_element_type=jnp.float32,
        )
        update = lax.all_to_all(update_slab, MODE, split_axis=1, concat_axis=0, tiled=True)
        squares = one_axis_at_a_time(jnp.sum(update * update), SPACE_MODE)
        damping = step_gain / jnp.sqrt(squares / total_cells + 1e-06)
        field = field + damping * update
    return field


def solution(mesh):
    torus = Mesh(mesh.devices.reshape(8, 2, 4, 4), ("space_0", "space_1", "mode_0", "mode_1"))
    in_specs = (
        P(SPACE, MODE),
        P(SPACE, MODE),
        P(SPACE, None),
        P(SPACE, None),
        P(SPACE, None),
        P(MODE, None, None),
        P(),
        P(),
        P(),
    )
    out_specs = P(SPACE, MODE)
    return jax.shard_map(
        shards, mesh=torus, in_specs=in_specs, out_specs=out_specs, check_vma=False
    )
```

profile of v0, /device:TPU:2, one launch (start us, length us, event | category | flops | bytes accessed | tf_op | source)
XLA Modules:
  0.0 349.0 jit_solution(4169821131279760908)
XLA Ops:
  17.1 7.5 %all-to-all-start.1 = ((bf16[16,32,128]{2,1,0:T(8,128)(2,1)}), bf16[16,32,128]{2,1,0:T(8,128)(2,1)S(1)}, u32[]{:S(2)}, u32[]{:S(2)}) async-start(bf16[16,32,128]{2,1,0:T(8,128)(2,1)} %bitcast.11), calls=%async_computation.1 | async-start | bytes 262144 | tf_op jit(solution)/shard_map/all_to_all | solution.py:77
  32.7 5.0 %all-to-all-start = ((f32[16,32,128]{2,1,0:T(8,128)}), f32[16,32,128]{2,1,0:T(8,128)S(1)}, u32[]{:S(2)}, u32[]{:S(2)}) async-start(f32[16,32,128]{2,1,0:T(8,128)} %bitcast.5), calls=%async_computation | async-start | bytes 524288 | tf_op jit(solution)/shard_map/all_to_all | solution.py:78
  37.7 32.6 %all-gather.2.cloned.1.call-done = bf16[128,128,128]{2,1,0:T(8,128)(2,1)} async-done(((bf16[8,128,128]{2,1,0:T(8,128)(2,1)}), bf16[128,128,128]{2,1,0:T(8,128)(2,1)}) %all-gather.2.cloned.1.call-update) | async-done | bytes 4194320 | tf_op jit(solution)/shard_map/all_gather | solution.py:54
  70.3 7.5 %convert_bitcast_fusion = bf16[16,128,16,128]{1,2,3,0:T(8,128)(2,1)} fusion(bf16[16,8,128,128]{3,2,1,0:T(8,128)(2,1)} %bitcast.187, s32[16,8]{1,0:T(8,128)S(1)} %copy.36, pred[16,8]{1,0:T(8,128)(4,1)S(1)} %iota_compare_fusion.1), kind=kOutput, calls=%fused_computation.12 | convolution fusion | flops 71307264 | bytes 12583552 | tf_op jit(solution)/shard_map/jsba,jst->jatb/dot_general | solution.py:60
  77.8 13.3 %copy.38 = bf16[16,128,16,128]{3,2,1,0:T(8,128)(2,1)} copy(bf16[16,128,16,128]{1,2,3,0:T(8,128)(2,1)} %convert_bitcast_fusion) | data formatting | bytes 16777216 | tf_op jit(solution)/shard_map/convert_element_type | solution.py:63
  91.1 9.8 %convolution_bitcast_fusion.2 = f32[4,16,8,128]{3,2,1,0:T(8,128)S(1)} fusion(bf16[2048,2048]{1,0:T(8,128)(2,1)} %param.17, bf16[256,8,16,128]{3,2,1,0:T(8,128)(2,1)} %bitcast.184, f32[16,32,128]{2,1,0:T(8,128)S(1)} %all-to-all-done, bf16[16,32,128]{2,1,0:T(8,128)(2,1)S(1)} %all-to-all-done.1), kind=kOutput, calls=%fused_computation.32 | convolution fusion | flops 537001984 | bytes 17432576 | tf_op jit(solution)/shard_map/dot_general | solution.py:83
  101.0 12.8 %all_to_all.153 = f32[32,16,128]{2,0,1:T(8,128)S(1)} all-to-all(f32[32,16,128]{2,0,1:T(8,128)S(1)} %bitcast.190), channel_id=1, replica_groups=mesh['space_0'=8,'space_1'=2,'mode_0'=4,'mode_1'=4] {'mode_0','mode_1'}, dimensions={1} | all-to-all | bytes 524288 | tf_op jit(solution)/shard_map/all_to_all | solution.py:89
  114.5 18.1 %psum.84 = f32[]{:T(128)} all-reduce(f32[]{:T(128)} %multiply_reduce_fusion.2), channel_id=1, replica_groups=mesh['space_0'=8,'space_1'=2,'mode_0'=4,'mode_1'=4] {'space_0'}, use_global_device_ids=true, to_apply=%region_1.0 | all-reduce | flops 1 | bytes 8 | tf_op jit(solution)/shard_map/psum | solution.py:33
  135.7 9.2 %psum.86 = f32[]{:T(128)} all-reduce(f32[]{:T(128)} %psum.85), channel_id=1, replica_groups=mesh['space_0'=8,'space_1'=2,'mode_0'=4,'mode_1'=4] {'mode_0'}, use_global_device_ids=true, to_apply=%region_3.0 | all-reduce | flops 1 | bytes 8 | tf_op jit(solution)/shard_map/psum | solution.py:33
  145.0 9.8 %psum.87 = f32[]{:T(128)} all-reduce(f32[]{:T(128)} %psum.86), channel_id=1, replica_groups=mesh['space_0'=8,'space_1'=2,'mode_0'=4,'mode_1'=4] {'mode_1'}, use_global_device_ids=true, to_apply=%region_4.0 | all-reduce | flops 1 | bytes 8 | tf_op jit(solution)/shard_map/psum | solution.py:33
  169.7 6.3 %all-to-all-done.4 = bf16[16,32,128]{2,1,0:T(8,128)(2,1)S(1)} async-done(((bf16[16,32,128]{2,1,0:T(8,128)(2,1)}), bf16[16,32,128]{2,1,0:T(8,128)(2,1)S(1)}, u32[]{:S(2)}, u32[]{:S(2)}) %all-to-all-start.4) | async-done | bytes 131104 | tf_op jit(solution)/shard_map/all_to_all | solution.py:77
  176.0 11.8 %all_to_all.154 = f32[16,32,128]{2,1,0:T(8,128)S(1)} all-to-all(f32[16,32,128]{2,1,0:T(8,128)S(1)} %bitcast.188), channel_id=1, replica_groups=mesh['space_0'=8,'space_1'=2,'mode_0'=4,'mode_1'=4] {'mode_0','mode_1'}, dimensions={0} | all-to-all | bytes 524288 | tf_op jit(solution)/shard_map/all_to_all | solution.py:78
  187.7 9.8 %convolution_bitcast_fusion.1 = f32[4,16,8,128]{3,2,1,0:T(8,128)S(1)} fusion(bf16[2048,2048]{1,0:T(8,128)(2,1)} %param.17, bf16[256,8,16,128]{3,2,1,0:T(8,128)(2,1)} %bitcast.185, f32[16,32,128]{2,1,0:T(8,128)S(1)} %all_to_all.154, bf16[16,32,128]{2,1,0:T(8,128)(2,1)S(1)} %all-to-all-done.4), kind=kOutput, calls=%fused_computation.28 | convolution fusion | flops 537001984 | bytes 17432576 | tf_op jit(solution)/shard_map/dot_general | solution.py:83
  197.5 11.6 %all_to_all.155 = f32[32,16,128]{2,0,1:T(8,128)S(1)} all-to-all(f32[32,16,128]{2,0,1:T(8,128)S(1)} %bitcast.191), channel_id=1, replica_groups=mesh['space_0'=8,'space_1'=2,'mode_0'=4,'mode_1'=4] {'mode_0','mode_1'}, dimensions={1} | all-to-all | bytes 524288 | tf_op jit(solution)/shard_map/all_to_all | solution.py:89
  209.8 15.6 %psum.88 = f32[]{:T(128)} all-reduce(f32[]{:T(128)} %multiply_reduce_fusion.1), channel_id=1, replica_groups=mesh['space_0'=8,'space_1'=2,'mode_0'=4,'mode_1'=4] {'space_0'}, use_global_device_ids=true, to_apply=%region_6.0 | all-reduce | flops 1 | bytes 8 | tf_op jit(solution)/shard_map/psum | solution.py:33
  228.5 9.2 %psum.90 = f32[]{:T(128)} all-reduce(f32[]{:T(128)} %psum.89), channel_id=1, replica_groups=mesh['space_0'=8,'space_1'=2,'mode_0'=4,'mode_1'=4] {'mode_0'}, use_global_device_ids=true, to_apply=%region_8.0 | all-reduce | flops 1 | bytes 8 | tf_op jit(solution)/shard_map/psum | solution.py:33
  237.7 9.8 %psum.91 = f32[]{:T(128)} all-reduce(f32[]{:T(128)} %psum.90), channel_id=1, replica_groups=mesh['space_0'=8,'space_1'=2,'mode_0'=4,'mode_1'=4] {'mode_1'}, use_global_device_ids=true, to_apply=%region_9.0 | all-reduce | flops 1 | bytes 8 | tf_op jit(solution)/shard_map/psum | solution.py:33
  262.3 6.8 %all-to-all-done.7 = bf16[16,32,128]{2,1,0:T(8,128)(2,1)S(1)} async-done(((bf16[16,32,128]{2,1,0:T(8,128)(2,1)}), bf16[16,32,128]{2,1,0:T(8,128)(2,1)S(1)}, u32[]{:S(2)}, u32[]{:S(2)}) %all-to-all-start.7) | async-done | bytes 131104 | tf_op jit(solution)/shard_map/all_to_all | solution.py:77
  269.1 11.8 %all_to_all.156 = f32[16,32,128]{2,1,0:T(8,128)S(1)} all-to-all(f32[16,32,128]{2,1,0:T(8,128)S(1)} %bitcast.189), channel_id=1, replica_groups=mesh['space_0'=8,'space_1'=2,'mode_0'=4,'mode_1'=4] {'mode_0','mode_1'}, dimensions={0} | all-to-all | bytes 524288 | tf_op jit(solution)/shard_map/all_to_all | solution.py:78
  280.9 9.8 %convolution_bitcast_fusion = f32[4,16,8,128]{3,2,1,0:T(8,128)S(1)} fusion(bf16[2048,2048]{1,0:T(8,128)(2,1)} %param.17, bf16[256,8,16,128]{3,2,1,0:T(8,128)(2,1)} %bitcast.186, f32[16,32,128]{2,1,0:T(8,128)S(1)} %all_to_all.156, bf16[16,32,128]{2,1,0:T(8,128)(2,1)S(1)} %all-to-all-done.7), kind=kOutput, calls=%fused_computation.24 | convolution fusion | flops 537001984 | bytes 17432576 | tf_op jit(solution)/shard_map/dot_general | solution.py:83
  290.7 11.6 %all_to_all.157 = f32[32,16,128]{2,0,1:T(8,128)S(1)} all-to-all(f32[32,16,128]{2,0,1:T(8,128)S(1)} %bitcast.192), channel_id=1, replica_groups=mesh['space_0'=8,'space_1'=2,'mode_0'=4,'mode_1'=4] {'mode_0','mode_1'}, dimensions={1} | all-to-all | bytes 524288 | tf_op jit(solution)/shard_map/all_to_all | solution.py:89
  302.9 15.7 %psum.92 = f32[]{:T(128)} all-reduce(f32[]{:T(128)} %multiply_reduce_fusion), channel_id=1, replica_groups=mesh['space_0'=8,'space_1'=2,'mode_0'=4,'mode_1'=4] {'space_0'}, use_global_device_ids=true, to_apply=%region_11.0 | all-reduce | flops 1 | bytes 8 | tf_op jit(solution)/shard_map/psum | solution.py:33
  321.7 9.2 %psum.94 = f32[]{:T(128)} all-reduce(f32[]{:T(128)} %psum.93), channel_id=1, replica_groups=mesh['space_0'=8,'space_1'=2,'mode_0'=4,'mode_1'=4] {'mode_0'}, use_global_device_ids=true, to_apply=%region_13.0 | all-reduce | flops 1 | bytes 8 | tf_op jit(solution)/shard_map/psum | solution.py:33
  330.9 9.8 %psum.95 = f32[]{:T(128)} all-reduce(f32[]{:T(128)} %psum.94), channel_id=1, replica_groups=mesh['space_0'=8,'space_1'=2,'mode_0'=4,'mode_1'=4] {'mode_1'}, use_global_device_ids=true, to_apply=%region_14.0 | all-reduce | flops 1 | bytes 8 | tf_op jit(solution)/shard_map/psum | solution.py:33
  (62 shorter events, 58.9 us)
Async XLA Ops:
  6.5 18.1 %copy-start = (bf16[512,512]{1,0:T(8,128)(2,1)S(1)}, bf16[512,512]{1,0:T(8,128)(2,1)}, u32[]{:S(2)}) copy-start(bf16[512,512]{1,0:T(8,128)(2,1)} %param.11) | copy-start | bytes 1572868
  6.5 63.8 %all-gather.2.cloned.1.call-start = ((), (), s32[]{:S(2)}) async-start(), calls=%async_computation.9 | async-start | bytes 4456448 | tf_op jit(solution)/shard_map/all_gather | solution.py:54
  11.2 16.1 %collective-permute-start.1 = (bf16[128,128]{1,0:T(8,128)(2,1)S(1)}, bf16[128,128]{1,0:T(8,128)(2,1)S(1)}, u32[]{:S(2)}, u32[]{:S(2)}) collective-permute-start(bf16[128,128]{1,0:T(8,128)(2,1)S(1)} %gather_fusion.1), channel_id=1, source_target_pairs={{16,0},{32,16},{48,32},{64,48},{80,64},{96,80},{112,96},{128,112},... | collective-permute-start | bytes 98312 | tf_op jit(solution)/shard_map/ppermute | solution.py:24
  14.1 13.3 %collective-permute-start = (bf16[128,128]{1,0:T(8,128)(2,1)S(1)}, bf16[128,128]{1,0:T(8,128)(2,1)S(1)}, u32[]{:S(2)}, u32[]{:S(2)}) collective-permute-start(bf16[128,128]{1,0:T(8,128)(2,1)S(1)} %gather_fusion), channel_id=1, source_target_pairs={{0,16},{16,32},{32,48},{48,64},{64,80},{80,96},{96,112},{112,128},... | collective-permute-start | bytes 98312 | tf_op jit(solution)/shard_map/ppermute | solution.py:22
  17.1 15.6 %all-to-all-start.1 = ((bf16[16,32,128]{2,1,0:T(8,128)(2,1)}), bf16[16,32,128]{2,1,0:T(8,128)(2,1)S(1)}, u32[]{:S(2)}, u32[]{:S(2)}) async-start(bf16[16,32,128]{2,1,0:T(8,128)(2,1)} %bitcast.11), calls=%async_computation.1 | async-start | bytes 262144 | tf_op jit(solution)/shard_map/all_to_all | solution.py:77
  32.7 58.5 %all-to-all-start = ((f32[16,32,128]{2,1,0:T(8,128)}), f32[16,32,128]{2,1,0:T(8,128)S(1)}, u32[]{:S(2)}, u32[]{:S(2)}) async-start(f32[16,32,128]{2,1,0:T(8,128)} %bitcast.5), calls=%async_computation | async-start | bytes 524288 | tf_op jit(solution)/shard_map/all_to_all | solution.py:78
  91.1 53.8 %copy-start.3 = (f32[512,128]{1,0:T(8,128)S(1)}, f32[512,128]{1,0:T(8,128)}, u32[]{:S(2)}) copy-start(f32[512,128]{1,0:T(8,128)} %param.10) | copy-start | bytes 786436
  91.1 64.4 %copy-start.1 = (f32[512,128]{1,0:T(8,128)S(1)}, f32[512,128]{1,0:T(8,128)}, u32[]{:S(2)}) copy-start(f32[512,128]{1,0:T(8,128)} %param.9) | copy-start | bytes 786436
  91.1 78.2 %copy-start.2 = (bf16[512,256]{1,0:T(8,128)(2,1)S(1)}, bf16[512,256]{1,0:T(8,128)(2,1)}, u32[]{:S(2)}) copy-start(bf16[512,256]{1,0:T(8,128)(2,1)} %param.12) | copy-start | bytes 786436
  159.4 9.9 %collective-permute-start.3 = (bf16[128,128]{1,0:T(8,128)(2,1)S(1)}, bf16[128,128]{1,0:T(8,128)(2,1)S(1)}, u32[]{:S(2)}, u32[]{:S(2)}) collective-permute-start(bf16[128,128]{1,0:T(8,128)(2,1)S(1)} %gather_fusion.3), channel_id=1, source_target_pairs={{16,0},{32,16},{48,32},{64,48},{80,64},{96,80},{112,96},{128,112},... | collective-permute-start | bytes 98312 | tf_op jit(solution)/shard_map/ppermute | solution.py:24
  160.7 8.6 %collective-permute-start.2 = (bf16[128,128]{1,0:T(8,128)(2,1)S(1)}, bf16[128,128]{1,0:T(8,128)(2,1)S(1)}, u32[]{:S(2)}, u32[]{:S(2)}) collective-permute-start(bf16[128,128]{1,0:T(8,128)(2,1)S(1)} %gather_fusion.2), channel_id=1, source_target_pairs={{0,16},{16,32},{32,48},{48,64},{64,80},{80,96},{96,112},{112,128},... | collective-permute-start | bytes 98312 | tf_op jit(solution)/shard_map/ppermute | solution.py:22
  165.0 11.0 %all-to-all-start.4 = ((bf16[16,32,128]{2,1,0:T(8,128)(2,1)}), bf16[16,32,128]{2,1,0:T(8,128)(2,1)S(1)}, u32[]{:S(2)}, u32[]{:S(2)}) async-start(bf16[16,32,128]{2,1,0:T(8,128)(2,1)} %bitcast.19), calls=%async_computation.4 | async-start | bytes 262144 | tf_op jit(solution)/shard_map/all_to_all | solution.py:77
  252.1 9.9 %collective-permute-start.5 = (bf16[128,128]{1,0:T(8,128)(2,1)S(1)}, bf16[128,128]{1,0:T(8,128)(2,1)S(1)}, u32[]{:S(2)}, u32[]{:S(2)}) collective-permute-start(bf16[128,128]{1,0:T(8,128)(2,1)S(1)} %gather_fusion.5), channel_id=1, source_target_pairs={{16,0},{32,16},{48,32},{64,48},{80,64},{96,80},{112,96},{128,112},... | collective-permute-start | bytes 98312 | tf_op jit(solution)/shard_map/ppermute | solution.py:24
  253.3 8.6 %collective-permute-start.4 = (bf16[128,128]{1,0:T(8,128)(2,1)S(1)}, bf16[128,128]{1,0:T(8,128)(2,1)S(1)}, u32[]{:S(2)}, u32[]{:S(2)}) collective-permute-start(bf16[128,128]{1,0:T(8,128)(2,1)S(1)} %gather_fusion.4), channel_id=1, source_target_pairs={{0,16},{16,32},{32,48},{48,64},{64,80},{80,96},{96,112},{112,128},... | collective-permute-start | bytes 98312 | tf_op jit(solution)/shard_map/ppermute | solution.py:22
  257.6 11.5 %all-to-all-start.7 = ((bf16[16,32,128]{2,1,0:T(8,128)(2,1)}), bf16[16,32,128]{2,1,0:T(8,128)(2,1)S(1)}, u32[]{:S(2)}, u32[]{:S(2)}) async-start(bf16[16,32,128]{2,1,0:T(8,128)(2,1)} %bitcast.26), calls=%async_computation.7 | async-start | bytes 262144 | tf_op jit(solution)/shard_map/all_to_all | solution.py:77
Sparse Core Ops, SparseCore 0:
  9.8 60.4 all-gather.1
where the time goes:
time: 351 us; the launch traced here: 349 us
  blocking collectives  175 us (50%)
  waiting for transfers between devices  49.9 us (14%)
  matrix products  42.9 us (12%)
  starting transfers between devices  34.1 us (10%)
  local copies, waits for them, and re-layouts  24 us (7%)
  between operations  15.7 us (4%)
  other arithmetic  7.31 us (2%)
    psum x12, blocking collectives, one_axis_at_a_time(): value = lax.psum(value, axis)  116 us
    all_to_all x3, blocking collectives, shards(): lax.all_to_all(update_slab, MODE, split_axis=1, concat_axis=0, tiled=True)  36 us
    all_gather x1, waiting for transfers between devices, shards(): slab_tables = lax.all_gather(chaos_vals, MODE, axis=0, tiled=True)  32.6 us
    dot_general x3, matrix products, shards(): lax.dot_general(residual_slab, mean_inverse, (((1,), (1,)), ((), ())), pr...  29.3 us
    all_to_all x2, blocking collectives, shards(): lax.all_to_all(forcing - spatial, MODE, split_axis=0, concat_axis=1, tile...  23.5 us
    all_to_all x3, waiting for transfers between devices, shards(): lax.all_to_all(field_bf, MODE, split_axis=0, concat_axis=1, tiled=True)  16.5 us
    all_to_all x3, starting transfers between devices, shards(): lax.all_to_all(field_bf, MODE, split_axis=0, concat_axis=1, tiled=True)  16.1 us
    convert_element_type x1, local copies, waits for them, and re-layouts, shards(): full_table.astype(jnp.bfloat16)  13.3 us
  transfers between devices with their start and end apart: 11, of which 4 were waited for; matrix products, arithmetic and copies ran while one was open for 10% of the time, Pallas kernels for 0%

commit v1 on v0

--- a/solution.py
+++ b/solution.py
@@ -30,7 +30,8 @@
 
 def one_axis_at_a_time(value, axes):
     for axis in axes:
-        value = lax.psum(value, axis)
+        tall = lax.all_gather(value, axis)
+        value = jnp.sum(tall, axis=0)
     return value
 
 

time: 351 us -> 369 us (1.051)
  blocking collectives: 175 us -> 155 us
  local copies, waits for them, and re-layouts: 24 us -> 43.3 us
  other arithmetic: 7.31 us -> 14.6 us
  waiting for transfers between devices: 49.9 us -> 56.5 us
  starting transfers between devices: 34.1 us -> 39.8 us
    psum x12 -> x0, blocking collectives: 116 us -> none  [one_axis_at_a_time(): value = lax.psum(value, axis)]
    unnamed x0 -> x12, blocking collectives: none -> 108 us
    unnamed x10 -> x46, local copies, waits for them, and re-layouts: 0.9 us -> 19.5 us
    all_to_all x3 -> x2, blocking collectives: 36 us -> 23.2 us  [shards(): lax.all_to_all(update_slab, MODE, split_axis=1, concat_axis=0, tiled=True)]
    reduce_sum x0 -> x12, other arithmetic: none -> 7.24 us  [one_axis_at_a_time(): value = jnp.sum(tall, axis=0)]
    all_to_all x0 -> x1, waiting for transfers between devices: none -> 6.62 us  [shards(): lax.all_to_all(update_slab, MODE, split_axis=1, concat_axis=0, tiled=True)]
    all_to_all x0 -> x1, starting transfers between devices: none -> 5.72 us  [shards(): lax.all_to_all(update_slab, MODE, split_axis=1, concat_axis=0, tiled=True)]
  transfers between devices with their start and end apart: 11 -> 12, of which waited for: 4 -> 5; matrix products, arithmetic and copies ran while one was open for 10% -> 9% of each run, Pallas kernels for 0% -> 0%
where the time goes in v1:
time: 369 us; the launch traced here: 367 us
  blocking collectives  155 us (42%)
  waiting for transfers between devices  56.5 us (15%)
  local copies, waits for them, and re-layouts  43.3 us (12%)
  matrix products  42.9 us (12%)
  starting transfers between devices  39.8 us (11%)
  between operations  15.8 us (4%)
  other arithmetic  14.6 us (4%)
    unnamed x12, blocking collectives  108 us
    all_gather x1, waiting for transfers between devices, shards(): slab_tables = lax.all_gather(chaos_vals, MODE, axis=0, tiled=True)  32.6 us
    dot_general x3, matrix products, shards(): lax.dot_general(residual_slab, mean_inverse, (((1,), (1,)), ((), ())), pr...  29.4 us
    all_to_all x2, blocking collectives, shards(): lax.all_to_all(forcing - spatial, MODE, split_axis=0, concat_axis=1, tile...  23.5 us
    all_to_all x2, blocking collectives, shards(): lax.all_to_all(update_slab, MODE, split_axis=1, concat_axis=0, tiled=True)  23.2 us
    unnamed x46, local copies, waits for them, and re-layouts  19.5 us
    all_to_all x3, waiting for transfers between devices, shards(): lax.all_to_all(field_bf, MODE, split_axis=0, concat_axis=1, tiled=True)  16.5 us
    all_to_all x3, starting transfers between devices, shards(): lax.all_to_all(field_bf, MODE, split_axis=0, concat_axis=1, tiled=True)  16.1 us
  transfers between devices with their start and end apart: 12, of which 5 were waited for; matrix products, arithmetic and copies ran while one was open for 9% of the time, Pallas kernels for 0%

profile of v1, /device:TPU:2, one launch (start us, length us, event | category | flops | bytes accessed | tf_op | source)
XLA Modules:
  0.0 367.5 jit_solution(15394727999012768118)
XLA Ops:
  17.1 7.5 %all-to-all-start.1 = ((bf16[16,32,128]{2,1,0:T(8,128)(2,1)}), bf16[16,32,128]{2,1,0:T(8,128)(2,1)S(1)}, u32[]{:S(2)}, u32[]{:S(2)}) async-start(bf16[16,32,128]{2,1,0:T(8,128)(2,1)} %bitcast.11), calls=%async_computation.1 | async-start | bytes 262144 | tf_op jit(solution)/shard_map/all_to_all | solution.py:78
  37.7 32.6 %all-gather.2.cloned.1.call-done = bf16[128,128,128]{2,1,0:T(8,128)(2,1)} async-done(((bf16[8,128,128]{2,1,0:T(8,128)(2,1)}), bf16[128,128,128]{2,1,0:T(8,128)(2,1)}) %all-gather.2.cloned.1.call-update) | async-done | bytes 4194320 | tf_op jit(solution)/shard_map/all_gather | solution.py:55
  70.3 7.5 %convert_bitcast_fusion = bf16[16,128,16,128]{1,2,3,0:T(8,128)(2,1)} fusion(bf16[16,8,128,128]{3,2,1,0:T(8,128)(2,1)} %bitcast.203, s32[16,8]{1,0:T(8,128)S(1)} %copy.36, pred[16,8]{1,0:T(8,128)(4,1)S(1)} %iota_compare_fusion.1), kind=kOutput, calls=%fused_computation.12 | convolution fusion | flops 71307264 | bytes 12583552 | tf_op jit(solution)/shard_map/jsba,jst->jatb/dot_general | solution.py:61
  77.8 13.3 %copy.38 = bf16[16,128,16,128]{3,2,1,0:T(8,128)(2,1)} copy(bf16[16,128,16,128]{1,2,3,0:T(8,128)(2,1)} %convert_bitcast_fusion) | data formatting | bytes 16777216 | tf_op jit(solution)/shard_map/convert_element_type | solution.py:64
  91.2 9.9 %convolution_bitcast_fusion.2 = f32[4,16,8,128]{3,2,1,0:T(8,128)S(1)} fusion(bf16[2048,2048]{1,0:T(8,128)(2,1)} %param.17, bf16[256,8,16,128]{3,2,1,0:T(8,128)(2,1)} %bitcast.200, f32[16,32,128]{2,1,0:T(8,128)S(1)} %all-to-all-done, bf16[16,32,128]{2,1,0:T(8,128)(2,1)S(1)} %all-to-all-done.1), kind=kOutput, calls=%fused_computation.32 | convolution fusion | flops 537001984 | bytes 17432576 | tf_op jit(solution)/shard_map/dot_general | solution.py:84
  101.8 5.7 %all-to-all-start.2 = ((f32[32,16,128]{2,0,1:T(8,128)}), f32[32,16,128]{2,0,1:T(8,128)S(1)}, u32[]{:S(2)}, u32[]{:S(2)}) async-start(f32[32,16,128]{2,0,1:T(8,128)} %bitcast.199), calls=%async_computation.2 | async-start | bytes 524288 | tf_op jit(solution)/shard_map/all_to_all | solution.py:90
  108.2 6.6 %all-to-all-done.2 = f32[32,16,128]{2,0,1:T(8,128)S(1)} async-done(((f32[32,16,128]{2,0,1:T(8,128)}), f32[32,16,128]{2,0,1:T(8,128)S(1)}, u32[]{:S(2)}, u32[]{:S(2)}) %all-to-all-start.2) | async-done | bytes 262176 | tf_op jit(solution)/shard_map/all_to_all | solution.py:90
  117.4 17.4 %all-reduce = f32[8]{0:T(128)S(1)} all-reduce(f32[8]{0:T(128)S(1)} %dynamic-update-slice), channel_id=1, replica_groups=mesh['space_0'=8,'space_1'=2,'mode_0'=4,'mode_1'=4] {'space_0'}, use_global_device_ids=true, to_apply=%add | all-reduce | flops 8 | bytes 64
  142.4 8.6 %all-reduce.2 = f32[4]{0:T(128)S(1)} all-reduce(f32[4]{0:T(128)S(1)} %dynamic-update-slice.2), channel_id=1, replica_groups=mesh['space_0'=8,'space_1'=2,'mode_0'=4,'mode_1'=4] {'mode_0'}, use_global_device_ids=true, to_apply=%add.2 | all-reduce | flops 4 | bytes 32
  153.0 9.2 %all-reduce.3 = f32[4]{0:T(128)S(1)} all-reduce(f32[4]{0:T(128)S(1)} %dynamic-update-slice.3), channel_id=1, replica_groups=mesh['space_0'=8,'space_1'=2,'mode_0'=4,'mode_1'=4] {'mode_1'}, use_global_device_ids=true, to_apply=%add.3 | all-reduce | flops 4 | bytes 32
  177.5 6.3 %all-to-all-done.4 = bf16[16,32,128]{2,1,0:T(8,128)(2,1)S(1)} async-done(((bf16[16,32,128]{2,1,0:T(8,128)(2,1)}), bf16[16,32,128]{2,1,0:T(8,128)(2,1)S(1)}, u32[]{:S(2)}, u32[]{:S(2)}) %all-to-all-start.4) | async-done | bytes 131104 | tf_op jit(solution)/shard_map/all_to_all | solution.py:78
  183.8 11.8 %all_to_all.153 = f32[16,32,128]{2,1,0:T(8,128)S(1)} all-to-all(f32[16,32,128]{2,1,0:T(8,128)S(1)} %bitcast.204), channel_id=1, replica_groups=mesh['space_0'=8,'space_1'=2,'mode_0'=4,'mode_1'=4] {'mode_0','mode_1'}, dimensions={0} | all-to-all | bytes 524288 | tf_op jit(solution)/shard_map/all_to_all | solution.py:79
  195.6 9.8 %convolution_bitcast_fusion.1 = f32[4,16,8,128]{3,2,1,0:T(8,128)S(1)} fusion(bf16[2048,2048]{1,0:T(8,128)(2,1)} %param.17, bf16[256,8,16,128]{3,2,1,0:T(8,128)(2,1)} %bitcast.201, f32[16,32,128]{2,1,0:T(8,128)S(1)} %all_to_all.153, bf16[16,32,128]{2,1,0:T(8,128)(2,1)S(1)} %all-to-all-done.4), kind=kOutput, calls=%fused_computation.28 | convolution fusion | flops 537001984 | bytes 17432576 | tf_op jit(solution)/shard_map/dot_general | solution.py:84
  205.4 11.6 %all_to_all.154 = f32[32,16,128]{2,0,1:T(8,128)S(1)} all-to-all(f32[32,16,128]{2,0,1:T(8,128)S(1)} %bitcast.206), channel_id=1, replica_groups=mesh['space_0'=8,'space_1'=2,'mode_0'=4,'mode_1'=4] {'mode_0','mode_1'}, dimensions={1} | all-to-all | bytes 524288 | tf_op jit(solution)/shard_map/all_to_all | solution.py:90
  219.0 15.0 %all-reduce.4 = f32[8]{0:T(128)S(1)} all-reduce(f32[8]{0:T(128)S(1)} %dynamic-update-slice.4), channel_id=1, replica_groups=mesh['space_0'=8,'space_1'=2,'mode_0'=4,'mode_1'=4] {'space_0'}, use_global_device_ids=true, to_apply=%add.4 | all-reduce | flops 8 | bytes 64
  240.3 8.6 %all-reduce.6 = f32[4]{0:T(128)S(1)} all-reduce(f32[4]{0:T(128)S(1)} %dynamic-update-slice.6), channel_id=1, replica_groups=mesh['space_0'=8,'space_1'=2,'mode_0'=4,'mode_1'=4] {'mode_0'}, use_global_device_ids=true, to_apply=%add.6 | all-reduce | flops 4 | bytes 32
  250.9 9.2 %all-reduce.7 = f32[4]{0:T(128)S(1)} all-reduce(f32[4]{0:T(128)S(1)} %dynamic-update-slice.7), channel_id=1, replica_groups=mesh['space_0'=8,'space_1'=2,'mode_0'=4,'mode_1'=4] {'mode_1'}, use_global_device_ids=true, to_apply=%add.7 | all-reduce | flops 4 | bytes 32
  275.4 6.8 %all-to-all-done.7 = bf16[16,32,128]{2,1,0:T(8,128)(2,1)S(1)} async-done(((bf16[16,32,128]{2,1,0:T(8,128)(2,1)}), bf16[16,32,128]{2,1,0:T(8,128)(2,1)S(1)}, u32[]{:S(2)}, u32[]{:S(2)}) %all-to-all-start.7) | async-done | bytes 131104 | tf_op jit(solution)/shard_map/all_to_all | solution.py:78
  282.3 11.8 %all_to_all.155 = f32[16,32,128]{2,1,0:T(8,128)S(1)} all-to-all(f32[16,32,128]{2,1,0:T(8,128)S(1)} %bitcast.205), channel_id=1, replica_groups=mesh['space_0'=8,'space_1'=2,'mode_0'=4,'mode_1'=4] {'mode_0','mode_1'}, dimensions={0} | all-to-all | bytes 524288 | tf_op jit(solution)/shard_map/all_to_all | solution.py:79
  294.0 9.8 %convolution_bitcast_fusion = f32[4,16,8,128]{3,2,1,0:T(8,128)S(1)} fusion(bf16[2048,2048]{1,0:T(8,128)(2,1)} %param.17, bf16[256,8,16,128]{3,2,1,0:T(8,128)(2,1)} %bitcast.202, f32[16,32,128]{2,1,0:T(8,128)S(1)} %all_to_all.155, bf16[16,32,128]{2,1,0:T(8,128)(2,1)S(1)} %all-to-all-done.7), kind=kOutput, calls=%fused_computation.24 | convolution fusion | flops 537001984 | bytes 17432576 | tf_op jit(solution)/shard_map/dot_general | solution.py:84
  303.8 11.6 %all_to_all.156 = f32[32,16,128]{2,0,1:T(8,128)S(1)} all-to-all(f32[32,16,128]{2,0,1:T(8,128)S(1)} %bitcast.207), channel_id=1, replica_groups=mesh['space_0'=8,'space_1'=2,'mode_0'=4,'mode_1'=4] {'mode_0','mode_1'}, dimensions={1} | all-to-all | bytes 524288 | tf_op jit(solution)/shard_map/all_to_all | solution.py:90
  317.4 15.1 %all-reduce.8 = f32[8]{0:T(128)S(1)} all-reduce(f32[8]{0:T(128)S(1)} %dynamic-update-slice.8), channel_id=1, replica_groups=mesh['space_0'=8,'space_1'=2,'mode_0'=4,'mode_1'=4] {'space_0'}, use_global_device_ids=true, to_apply=%add.8 | all-reduce | flops 8 | bytes 64
  338.9 8.6 %all-reduce.10 = f32[4]{0:T(128)S(1)} all-reduce(f32[4]{0:T(128)S(1)} %dynamic-update-slice.10), channel_id=1, replica_groups=mesh['space_0'=8,'space_1'=2,'mode_0'=4,'mode_1'=4] {'mode_0'}, use_global_device_ids=true, to_apply=%add.10 | all-reduce | flops 4 | bytes 32
  349.4 9.2 %all-reduce.11 = f32[4]{0:T(128)S(1)} all-reduce(f32[4]{0:T(128)S(1)} %dynamic-update-slice.11), channel_id=1, replica_groups=mesh['space_0'=8,'space_1'=2,'mode_0'=4,'mode_1'=4] {'mode_1'}, use_global_device_ids=true, to_apply=%add.11 | all-reduce | flops 4 | bytes 32
  (111 shorter events, 88.6 us)
Async XLA Ops:
  6.5 18.1 %copy-start = (bf16[512,512]{1,0:T(8,128)(2,1)S(1)}, bf16[512,512]{1,0:T(8,128)(2,1)}, u32[]{:S(2)}) copy-start(bf16[512,512]{1,0:T(8,128)(2,1)} %param.11) | copy-start | bytes 1572868
  6.5 63.8 %all-gather.2.cloned.1.call-start = ((), (), s32[]{:S(2)}) async-start(), calls=%async_computation.9 | async-start | bytes 4456448 | tf_op jit(solution)/shard_map/all_gather | solution.py:55
  11.2 16.1 %collective-permute-start.1 = (bf16[128,128]{1,0:T(8,128)(2,1)S(1)}, bf16[128,128]{1,0:T(8,128)(2,1)S(1)}, u32[]{:S(2)}, u32[]{:S(2)}) collective-permute-start(bf16[128,128]{1,0:T(8,128)(2,1)S(1)} %gather_fusion.1), channel_id=1, source_target_pairs={{16,0},{32,16},{48,32},{64,48},{80,64},{96,80},{112,96},{128,112},... | collective-permute-start | bytes 98312 | tf_op jit(solution)/shard_map/ppermute | solution.py:24
  14.1 13.3 %collective-permute-start = (bf16[128,128]{1,0:T(8,128)(2,1)S(1)}, bf16[128,128]{1,0:T(8,128)(2,1)S(1)}, u32[]{:S(2)}, u32[]{:S(2)}) collective-permute-start(bf16[128,128]{1,0:T(8,128)(2,1)S(1)} %gather_fusion), channel_id=1, source_target_pairs={{0,16},{16,32},{32,48},{48,64},{64,80},{80,96},{96,112},{112,128},... | collective-permute-start | bytes 98312 | tf_op jit(solution)/shard_map/ppermute | solution.py:22
  17.1 15.6 %all-to-all-start.1 = ((bf16[16,32,128]{2,1,0:T(8,128)(2,1)}), bf16[16,32,128]{2,1,0:T(8,128)(2,1)S(1)}, u32[]{:S(2)}, u32[]{:S(2)}) async-start(bf16[16,32,128]{2,1,0:T(8,128)(2,1)} %bitcast.11), calls=%async_computation.1 | async-start | bytes 262144 | tf_op jit(solution)/shard_map/all_to_all | solution.py:78
  32.7 58.4 %all-to-all-start = ((f32[16,32,128]{2,1,0:T(8,128)}), f32[16,32,128]{2,1,0:T(8,128)S(1)}, u32[]{:S(2)}, u32[]{:S(2)}) async-start(f32[16,32,128]{2,1,0:T(8,128)} %bitcast.5), calls=%async_computation | async-start | bytes 524288 | tf_op jit(solution)/shard_map/all_to_all | solution.py:79
  91.1 16.4 %copy-start.3 = (f32[512,128]{1,0:T(8,128)S(1)}, f32[512,128]{1,0:T(8,128)}, u32[]{:S(2)}) copy-start(f32[512,128]{1,0:T(8,128)} %param.10) | copy-start | bytes 786436
  91.1 16.5 %copy-start.7 = (u32[256]{0:T(256)S(1)}, u32[256]{0:T(256)}, u32[]{:S(2)}) copy-start(u32[256]{0:T(256)} %constant.19) | copy-start | bytes 3076
  91.1 25.7 %copy-start.6 = (u32[256]{0:T(256)S(1)}, u32[256]{0:T(256)}, u32[]{:S(2)}) copy-start(u32[256]{0:T(256)} %constant.24) | copy-start | bytes 3076
  91.1 45.7 %copy-start.5 = (u32[256]{0:T(256)S(1)}, u32[256]{0:T(256)}, u32[]{:S(2)}) copy-start(u32[256]{0:T(256)} %constant.29) | copy-start | bytes 3076
  91.1 50.7 %copy-start.4 = (u32[256]{0:T(256)S(1)}, u32[256]{0:T(256)}, u32[]{:S(2)}) copy-start(u32[256]{0:T(256)} %constant.34) | copy-start | bytes 3076
  91.2 72.3 %copy-start.1 = (f32[512,128]{1,0:T(8,128)S(1)}, f32[512,128]{1,0:T(8,128)}, u32[]{:S(2)}) copy-start(f32[512,128]{1,0:T(8,128)} %param.9) | copy-start | bytes 786436
  91.2 86.0 %copy-start.2 = (bf16[512,256]{1,0:T(8,128)(2,1)S(1)}, bf16[512,256]{1,0:T(8,128)(2,1)}, u32[]{:S(2)}) copy-start(bf16[512,256]{1,0:T(8,128)(2,1)} %param.12) | copy-start | bytes 786436
  101.8 13.0 %all-to-all-start.2 = ((f32[32,16,128]{2,0,1:T(8,128)}), f32[32,16,128]{2,0,1:T(8,128)S(1)}, u32[]{:S(2)}, u32[]{:S(2)}) async-start(f32[32,16,128]{2,0,1:T(8,128)} %bitcast.199), calls=%async_computation.2 | async-start | bytes 524288 | tf_op jit(solution)/shard_map/all_to_all | solution.py:90
  167.3 9.9 %collective-permute-start.3 = (bf16[128,128]{1,0:T(8,128)(2,1)S(1)}, bf16[128,128]{1,0:T(8,128)(2,1)S(1)}, u32[]{:S(2)}, u32[]{:S(2)}) collective-permute-start(bf16[128,128]{1,0:T(8,128)(2,1)S(1)} %gather_fusion.3), channel_id=1, source_target_pairs={{16,0},{32,16},{48,32},{64,48},{80,64},{96,80},{112,96},{128,112},... | collective-permute-start | bytes 98312 | tf_op jit(solution)/shard_map/ppermute | solution.py:24
  168.6 8.6 %collective-permute-start.2 = (bf16[128,128]{1,0:T(8,128)(2,1)S(1)}, bf16[128,128]{1,0:T(8,128)(2,1)S(1)}, u32[]{:S(2)}, u32[]{:S(2)}) collective-permute-start(bf16[128,128]{1,0:T(8,128)(2,1)S(1)} %gather_fusion.2), channel_id=1, source_target_pairs={{0,16},{16,32},{32,48},{48,64},{64,80},{80,96},{96,112},{112,128},... | collective-permute-start | bytes 98312 | tf_op jit(solution)/shard_map/ppermute | solution.py:22
  172.8 11.0 %all-to-all-start.4 = ((bf16[16,32,128]{2,1,0:T(8,128)(2,1)}), bf16[16,32,128]{2,1,0:T(8,128)(2,1)S(1)}, u32[]{:S(2)}, u32[]{:S(2)}) async-start(bf16[16,32,128]{2,1,0:T(8,128)(2,1)} %bitcast.27), calls=%async_computation.4 | async-start | bytes 262144 | tf_op jit(solution)/shard_map/all_to_all | solution.py:78
  265.2 9.9 %collective-permute-start.5 = (bf16[128,128]{1,0:T(8,128)(2,1)S(1)}, bf16[128,128]{1,0:T(8,128)(2,1)S(1)}, u32[]{:S(2)}, u32[]{:S(2)}) collective-permute-start(bf16[128,128]{1,0:T(8,128)(2,1)S(1)} %gather_fusion.5), channel_id=1, source_target_pairs={{16,0},{32,16},{48,32},{64,48},{80,64},{96,80},{112,96},{128,112},... | collective-permute-start | bytes 98312 | tf_op jit(solution)/shard_map/ppermute | solution.py:24
  266.5 8.6 %collective-permute-start.4 = (bf16[128,128]{1,0:T(8,128)(2,1)S(1)}, bf16[128,128]{1,0:T(8,128)(2,1)S(1)}, u32[]{:S(2)}, u32[]{:S(2)}) collective-permute-start(bf16[128,128]{1,0:T(8,128)(2,1)S(1)} %gather_fusion.4), channel_id=1, source_target_pairs={{0,16},{16,32},{32,48},{48,64},{64,80},{80,96},{96,112},{112,128},... | collective-permute-start | bytes 98312 | tf_op jit(solution)/shard_map/ppermute | solution.py:22
  270.8 11.5 %all-to-all-start.7 = ((bf16[16,32,128]{2,1,0:T(8,128)(2,1)}), bf16[16,32,128]{2,1,0:T(8,128)(2,1)S(1)}, u32[]{:S(2)}, u32[]{:S(2)}) async-start(bf16[16,32,128]{2,1,0:T(8,128)(2,1)} %bitcast.38), calls=%async_computation.7 | async-start | bytes 262144 | tf_op jit(solution)/shard_map/all_to_all | solution.py:78
Sparse Core Ops, SparseCore 0:
  9.8 60.4 all-gather.1
